TPU v7x, 32 devices: a whole 2x2x4 slice. The times are simulated.
32 devices in a mesh: dp: 4 (over x, core), tm: 8 (over z, y).
Axes of the slice: x: 2, y: 2, z: 4, core: 2. Of those that a mesh axis runs over, the one named last changes fastest.
Arguments:
- latent: float32 [4, 64, 4096], P('dp', None, 'tm'), may hold values from -40 to 40
- target: float32 [4, 8192], P('dp', 'tm'), may hold values from -20 to 20
- up_kernel: float32 [4, 32, 64], replicated, may hold values from -0.5 to 0.5
- inner_kernel: float32 [3, 16, 32], replicated, may hold values from -0.625 to 0.625
- outer_kernel: float32 [32, 16], replicated, may hold values from -1.5 to 1.5
- out_kernel: float32 [7, 32], replicated, may hold values from -0.375 to 0.375
Outputs:
- latent_grad: float32 [4, 64, 4096], P('dp', None, 'tm')
- up_update: float32 [4, 32, 64], replicated
- inner_update: float32 [3, 16, 32], replicated
- outer_update: float32 [32, 16], replicated
- out_update: float32 [7, 32], replicated
All inputs are finite; a program needn't handle non-finite values.
Results may differ from a plain program's by a relative error of at most 0.0003.
Values sent between devices are 32-bit elements; how exact they have to be, the bound alone decides.
No kernel may reach another device: no remote copies, remote signals or barrier semaphores. Data moves between devices by JAX's collectives and lax.ppermute only.
A program may use at most 64 MiB of HBM per device.

v0:
```python
import jax
import jax.numpy as jnp
from jax import lax
from jax.sharding import PartitionSpec as P

MELS = 64
WIN_COARSE = 1024
WIN_FINE = 256
LOSS_WEIGHTS = (0.25, 0.5, 0.5)


def padded_2(cells, sides, width):
    for axis, dim in sides:
        count = lax.axis_size(axis)
        ends = count - 1
        head = lax.slice_in_dim(cells, 0, width, axis=dim)
        tail = lax.slice_in_dim(cells, cells.shape[dim] - width, cells.shape[dim], axis=dim)
        cells = jnp.concatenate(
            [
                lax.ppermute(tail, axis, [(i, (i + 1) % count) for i in range(ends)]),
                cells,
                lax.ppermute(head, axis, [((i + 1) % count, i) for i in range(ends)]),
            ],
            axis=dim,
        )
    return cells


def from_behind(x, axis, by):
    peers = lax.axis_size(axis)
    pairs = [(i, i + by) for i in range(peers) if 0 <= i + by < peers]
    return lax.ppermute(x, axis, pairs)


def product(form, left, right):
    return jnp.einsum(
        form, left, right, precision=lax.Precision.HIGHEST, preferred_element_type=jnp.float32
    )


def mel_bank(window, mel_count):
    half_window = window // 2
    top_mel = 2595.0 * jnp.log10(1.0 + 12000.0 / 700.0)
    points = (jnp.arange(mel_count + 1, dtype=jnp.float32) + 1.0) / (mel_count + 2.0) * top_mel
    centers = 700.0 * (jnp.power(10.0, points / 2595.0) - 1.0) / 12000.0 * half_window
    spacing = jnp.maximum(centers[1:] - centers[:-1], 1.0)
    places = jnp.arange(half_window, dtype=jnp.float32)[:, None]
    return jnp.maximum(0.0, 1.0 - jnp.abs(places - centers[None, :mel_count]) / spacing[None, :])


def dft_table(window):
    half_window = window // 2
    sample = jnp.arange(window, dtype=jnp.int32)[:, None]
    freq_index = jnp.arange(half_window, dtype=jnp.int32)[None, :]
    angles = (sample * freq_index % window).astype(jnp.float32) * (2.0 * jnp.pi / window)
    hann_taper = 0.5 - 0.5 * jnp.cos(sample.astype(jnp.float32) * (2.0 * jnp.pi / window))
    return jnp.concatenate([hann_taper * jnp.cos(angles), -hann_taper * jnp.sin(angles)], axis=1)


def framed(signal, window, frame_count):
    hop_size = window // 4
    blocks = signal.reshape(signal.shape[:-1] + (frame_count + 3, hop_size))
    return jnp.concatenate(
        [blocks[..., offset : offset + frame_count, :] for offset in range(4)], axis=-1
    )


def mel_energy(signal, window, frame_count):
    frames = framed(signal, window, frame_count)
    spectra = product("...nf,fk->...nk", frames, dft_table(window))
    half_window = window // 2
    energy = spectra[..., :half_window] ** 2 + spectra[..., half_window:] ** 2
    return product("...nk,km->...nm", energy, mel_bank(window, MELS))


def spectral_loss(signal, target_mel, window, frame_count):
    level = jnp.sqrt(mel_energy(signal, window, frame_count) + 1.0)
    return jnp.sum((level - jnp.sqrt(target_mel + 1.0)) ** 2)


def elu_slope(values):
    return jnp.where(values > 0, 1.0, jnp.exp(jnp.minimum(values, 0.0)))


def apply_mask(values, mask):
    return values * mask


def upsample_forward(values, kernel, stride, previous):
    lagged = jnp.concatenate([previous, values[:, :, :-1]], axis=2)
    phases = product("pij,bjm->bimp", kernel[:stride], values) + product(
        "pij,bjm->bimp", kernel[stride:], lagged
    )
    return (phases.reshape(phases.shape[0], phases.shape[1], -1), lagged)


def taps_forward(padded, kernel, length):
    summed = product("oi,bil->bol", kernel[0], padded[:, :, :length])
    for offset in range(1, kernel.shape[0]):
        summed = summed + product(
            "oi,bil->bol", kernel[offset], padded[:, :, offset : offset + length]
        )
    return summed


def decode_forward(activated, weights, movers, clip_mask):
    up_kernel, inner_kernel, outer_kernel, out_kernel = weights
    lend_frame, border_inner, border_output = movers
    upper, lagged = upsample_forward(activated, up_kernel, 2, lend_frame(activated[:, :, -1:]))
    upper = apply_mask(upper, clip_mask)
    padded_inner = border_inner(jax.nn.elu(upper))
    inner_out = taps_forward(padded_inner, inner_kernel, upper.shape[2])
    hidden = jax.nn.elu(inner_out)
    mixed = apply_mask(upper + product("oi,bil->bol", outer_kernel, hidden), clip_mask)
    padded_output = border_output(jax.nn.elu(mixed))
    waveform = taps_forward(padded_output, out_kernel[:, None, :], upper.shape[2])[:, 0, :]
    return (waveform, (upper, lagged, padded_inner, inner_out, hidden, mixed, padded_output))


def taps_backward(grad_out, padded, kernel, length, keep):
    tap_count = kernel.shape[0]
    row_grad = apply_mask(grad_out, keep)
    kernel_rows = jnp.stack(
        [
            product("nbol,bil->nboi", row_grad, padded[:, :, offset : offset + length])
            for offset in range(tap_count)
        ],
        axis=2,
    )
    spread = jnp.zeros(grad_out.shape[:2] + (kernel.shape[2], length + tap_count - 1), jnp.float32)
    for offset in range(tap_count):
        moved = product("oi,nbol->nbil", kernel[offset], grad_out)
        spread = spread + jnp.pad(moved, ((0, 0), (0, 0), (0, 0), (offset, tap_count - 1 - offset)))
    return (kernel_rows, spread)


def rims_backward(spread, rim_width):
    interior = spread[..., rim_width:-rim_width]
    return interior


def residual_backward(
    grad_mixed, upper, padded, inner_out, hidden, inner_kernel, outer_kernel, keep
):
    length = upper.shape[-1]
    outer_rows = product("nbol,bil->nboi", apply_mask(grad_mixed, keep), hidden)
    grad_inner = product("oi,nbol->nbil", outer_kernel, grad_mixed) * elu_slope(inner_out)
    inner_rows, spread = taps_backward(grad_inner, padded, inner_kernel, length, keep)
    grad_rectified = rims_backward(spread, 1)
    return (grad_mixed + grad_rectified * elu_slope(upper), inner_rows, outer_rows)


def upsample_backward(grad_upper, values, lagged, kernel, stride, keep):
    phase_shape = grad_upper.shape[:3] + (values.shape[-1], stride)
    grad_phase = grad_upper.reshape(phase_shape)
    row_phase = apply_mask(grad_upper, keep).reshape(phase_shape)
    first_rows = product("nbimp,bjm->nbpij", row_phase, values)
    second_rows = product("nbimp,bjm->nbpij", row_phase, lagged)
    grad_values = product("pij,nbimp->nbjm", kernel[:stride], grad_phase)
    grad_lagged = product("pij,nbimp->nbjm", kernel[stride:], grad_phase)
    arrived = jnp.zeros_like(grad_lagged[..., :1])
    grad_values = grad_values + jnp.concatenate([grad_lagged[..., 1:], arrived], axis=-1)
    return (grad_values, jnp.concatenate([first_rows, second_rows], axis=2))


def local(latent, target, up_kernel, inner_kernel, outer_kernel, out_kernel):
    weights = (up_kernel, inner_kernel, outer_kernel, out_kernel)
    clips_here = target.shape[0]
    samples = target.shape[1]
    frames_here = latent.shape[2]
    latent_in = padded_2(latent, (("tm", 2),), 4)
    start_frame = 4
    margin = 8

    def lend_frame(edge):
        return jnp.zeros_like(edge)

    def border_inner(values):
        return jnp.pad(values, ((0, 0), (0, 0), (1, 1)))

    def border_output(values):
        return jnp.pad(values, ((0, 0), (0, 0), (3, 3)))

    shard_index = lax.axis_index("tm")
    shard_total = lax.axis_size("tm")
    wide_length = samples + 2 * margin
    local_places = jnp.arange(wide_length, dtype=jnp.int32)
    clip_places = samples * shard_index - margin + local_places
    clip_mask = ((clip_places >= 0) & (clip_places < samples * shard_total)).astype(jnp.float32)
    keep_rows = ((local_places >= margin) & (local_places < margin + samples)).astype(jnp.float32)
    activated = jax.nn.elu(latent_in)
    wave_all, saved = decode_forward(
        activated, weights, (lend_frame, border_inner, border_output), clip_mask
    )
    upper, lagged, padded_inner, inner_out, hidden, mixed, padded_output = saved
    waveform = wave_all[:, margin : margin + samples]
    tail_length = 3 * WIN_COARSE // 4
    wave_next, target_next = from_behind(
        (waveform[:, :tail_length], target[:, :tail_length]), "tm", -1
    )
    long_wave = jnp.concatenate([waveform, wave_next], axis=1)
    long_target = jnp.concatenate([target, target_next], axis=1)
    gradients = [2.0 * (waveform - target)]
    tails = []
    for window in (WIN_COARSE, WIN_FINE):
        hop_size = window // 4
        frame_count = samples // hop_size
        span = samples + 3 * hop_size
        target_mel = mel_energy(long_target[:, :span], window, frame_count)

        def scale_loss(signal):
            return spectral_loss(signal, target_mel, window, frame_count)

        local_grad = jax.grad(scale_loss)(long_wave[:, :span])
        gradients.append(local_grad[:, :samples])
        tails.append(jnp.pad(local_grad[:, samples:], ((0, 0), (0, tail_length - 3 * hop_size))))
    coarse_in, fine_in = from_behind((tails[0], tails[1]), "tm", 1)
    gradients[1] = gradients[1] + jnp.pad(coarse_in, ((0, 0), (0, samples - tail_length)))
    gradients[2] = gradients[2] + jnp.pad(fine_in, ((0, 0), (0, samples - tail_length)))
    squares = jnp.stack([jnp.sum(member * member, axis=1) for member in gradients], axis=1)
    squares = lax.psum(squares, "tm")
    total_samples = samples * lax.axis_size("tm")
    grad_scale = jnp.asarray(LOSS_WEIGHTS, jnp.float32)[None, :] / jnp.sqrt(
        squares / total_samples + 1e-06
    )
    streams = (
        gradients[0] * grad_scale[:, 0, None]
        + gradients[1] * grad_scale[:, 1, None]
        + gradients[2] * grad_scale[:, 2, None]
    )[None]
    row_weights = jnp.ones((1, clips_here), jnp.float32)
    streams_wide = padded_2(streams, (("tm", 2),), 8)
    wave_length = mixed.shape[2]
    out_taps = out_kernel[:, None, :]
    kernel_rows_out, spread_out = taps_backward(
        streams_wide[:, :, None, :], padded_output, out_taps, wave_length, keep_rows
    )
    out_rows = kernel_rows_out[:, :, :, 0, :]
    grad_final = rims_backward(spread_out, 3)
    grad_mixed = apply_mask(grad_final * elu_slope(mixed), clip_mask)
    grad_upper, inner_rows, outer_rows = residual_backward(
        grad_mixed, upper, padded_inner, inner_out, hidden, inner_kernel, outer_kernel, keep_rows
    )
    grad_activated, up_rows = upsample_backward(
        apply_mask(grad_upper, clip_mask), activated, lagged, up_kernel, 2, keep_rows
    )
    grad_latent_rows = grad_activated[..., start_frame : start_frame + frames_here] * elu_slope(
        latent
    )
    latent_grad = product("nb,nbcm->bcm", row_weights, grad_latent_rows)
    local_totals = [
        product("nb,nb...->...", row_weights, member)
        for member in (up_rows, inner_rows, outer_rows, out_rows)
    ]
    param_count = sum((member.size for member in local_totals))
    summed = lax.psum(
        (local_totals[0], local_totals[1], local_totals[2], local_totals[3]), ("dp", "tm")
    )
    squares_all = sum((jnp.sum(member * member) for member in summed))
    factor = jnp.minimum(1.0, 1.0 / jnp.sqrt(squares_all / param_count + 1e-06))
    updates = [member * factor for member in summed]
    return (latent_grad, updates[0], updates[1], updates[2], updates[3])


def solution(mesh):
    placed = (P("dp", None, "tm"), P("dp", "tm"), P(), P(), P(), P())
    return jax.shard_map(
        local,
        mesh=mesh,
        in_specs=placed,
        out_specs=(P("dp", None, "tm"), P(), P(), P(), P()),
        check_vma=False,
    )
```

profile of v0, /device:TPU:0, one launch (start us, length us, event | category | flops | bytes accessed | tf_op | source)
XLA Modules:
  0.0 188.2 jit_solution(7671481007626582187)
XLA Ops:
  4.1 5.5 %collective-permute-start = (f32[1,64,4]{2,1,0:T(8,128)S(1)}, f32[1,64,4]{2,1,0:T(8,128)S(1)}, u32[]{:S(2)}, u32[]{:S(2)}) collective-permute-start(f32[1,64,4]{2,1,0:T(8,128)S(1)} %get-tuple-element.15), channel_id=1, source_target_pairs={{0,1},{1,2},{2,3},{3,4},{4,5},{5,6},{6,7},{8,9},{9,10},{10,11},{11... | collective-permute-start | bytes 3080 | tf_op jit(solution)/shard_map/ppermute | solution.py:20
  9.6 1.3 collective-permute-start.1
  12.3 1.6 slice_bitcast_fusion.6
  15.1 9.4 %sine_multiply_fusion = (f32[1024,512]{1,0:T(8,128)S(1)}, f32[1024,512]{1,0:T(8,128)}) fusion(f32[1024]{0:T(1024)S(1)} %fusion.218, f32[1024]{0:T(1024)S(1)} %multiply_subtract_fusion), kind=kLoop, calls=%fused_computation.21 | loop fusion | flops 8388608 | bytes 4202496 | tf_op jit(solution)/shard_map/jvp()/mul | solution.py:57
  31.4 1.3 compare_select_fusion.9
  39.6 2.0 %multiply_reduce_fusion.6 = (f32[]{:T(128)}, f32[1,1024]{1,0:T(1,128)}, f32[1,1792]{1,0:T(1,128)S(1)}) fusion(f32[1,1024]{1,0:T(1,128)} %param.8, f32[1,1040]{1,0:T(1,128)S(1)} %squeeze.11), kind=kLoop, calls=%fused_computation.340 | loop fusion | flops 4094 | bytes 16388 | tf_op jit(solution)/shard_map/reduce_sum | solution.py:220
  45.4 1.3 reduce.11
  48.0 1.4 reshape.970
  51.1 4.3 %fusion.15 = f32[1,4,1024]{2,1,0:T(4,128)} fusion(f32[1024,512]{1,0:T(8,128)S(1)} %get-tuple-element.77, f32[1024,512]{1,0:T(8,128)} %get-tuple-element.78, f32[1,4,256]{2,1,0:T(4,128)S(1)} %get-tuple-element.45, f32[1,4,256]{2,1,0:T(4,128)S(1)} %get-tuple-element.46, f32[1,4,256]{2,1,0:T(4,128)S(1)} %get-tuple-element.47, ...), kind=kOutput, calls=%fused_computation.33 | convolution fusion | flops 51392512 | bytes 4227072 | tf_op jit(solution)/shard_map/...nf,fk->...nk/dot_general | solution.py:36
  56.3 1.3 maximum_reduce_fusion
  57.6 1.3 reshape.959
  58.9 1.3 fusion.210
  60.2 1.4 reshape.967
  61.6 1.4 fusion.285
  69.7 1.4 reshape.974
  71.7 6.2 %collective-permute-start.5 = (f32[1,768]{1,0:T(1,128)S(1)}, f32[1,768]{1,0:T(1,128)S(1)}, u32[]{:S(2)}, u32[]{:S(2)}) collective-permute-start(f32[1,768]{1,0:T(1,128)S(1)} %pad.112), channel_id=1, source_target_pairs={{0,1},{1,2},{2,3},{3,4},{4,5},{5,6},{6,7},{8,9},{9,10},{10,11},{11... | collective-permute-start | bytes 9224 | tf_op jit(solution)/shard_map/ppermute | solution.py:32
  78.0 3.7 %fusion.14 = f32[1,4,1024]{2,1,0:T(4,128)S(1)} fusion(f32[1024,512]{1,0:T(8,128)S(1)} %get-tuple-element.77, f32[1024,512]{1,0:T(8,128)} %get-tuple-element.78, f32[1,4,256]{2,1,0:T(4,128)} %get-tuple-element.49, f32[1,4,256]{2,1,0:T(4,128)} %get-tuple-element.50, f32[1,4,256]{2,1,0:T(4,128)} %get-tuple-element.51, f32[1,4,256]{2,1,0:T(4,128)} %get-tuple-element.48), kind=kOutput, calls=%fused_computation.32 | convolution fusion | flops 51392512 | bytes 4227072 | tf_op jit(solution)/shard_map/jvp(...nf,fk->...nk)/dot_general | solution.py:36
  83.3 3.5 %fusion.16 = f32[1,4,1024]{2,1,0:T(4,128)S(1)} fusion(f32[1024,512]{1,0:T(8,128)S(1)} %get-tuple-element.77, f32[1024,512]{1,0:T(8,128)S(1)} %copy-done.1, f32[1,4,512]{2,1,0:T(4,128)S(1)} %get-tuple-element.18, f32[1,4,512]{2,1,0:T(4,128)S(1)} %get-tuple-element.17), kind=kOutput, calls=%fused_computation.34 | convolution fusion | flops 51384320 | bytes 4227072 | tf_op jit(solution)/shard_map/transpose(jvp(...nf,fk->...nk))/dot_general | solution.py:36
  86.9 5.0 %collective-permute-start.4 = (f32[1,768]{1,0:T(1,128)S(1)}, f32[1,768]{1,0:T(1,128)S(1)}, u32[]{:S(2)}, u32[]{:S(2)}) collective-permute-start(f32[1,768]{1,0:T(1,128)S(1)} %slice.347), channel_id=1, source_target_pairs={{0,1},{1,2},{2,3},{3,4},{4,5},{5,6},{6,7},{8,9},{9,10},{10,11},{11... | collective-permute-start | bytes 9224 | tf_op jit(solution)/shard_map/ppermute | solution.py:32
  93.8 2.0 %pad_maximum_fusion.16 = f32[1,3]{1,0:T(1,128)S(1)} fusion(f32[1,1]{1,0:T(1,128)} %bitcast.63, f32[1,1]{1,0:T(1,128)} %bitcast.53, f32[1,1]{1,0:T(1,128)} %bitcast.43), kind=kLoop, calls=%fused_computation.344 | loop fusion | flops 6 | bytes 24 | tf_op jit(solution)/shard_map/stack | solution.py:220
  96.0 22.0 %psum.35 = f32[1,3]{1,0:T(1,128)S(1)} all-reduce(f32[1,3]{1,0:T(1,128)S(1)} %pad_maximum_fusion.16), channel_id=1, replica_groups=mesh['dp'=4,'tm'=8] {'tm'}, use_global_device_ids=true, to_apply=%region_3.4 | all-reduce | flops 3 | bytes 24 | tf_op jit(solution)/shard_map/psum | solution.py:221
  119.8 2.1 %add_bitcast_fusion.1 = f32[1,1,1024]{2,1,0:T(1,128)S(1)} fusion(f32[1,1024]{1,0:T(1,128)S(1)} %get-tuple-element.14, f32[1,1024]{1,0:T(1,128)S(1)} %get-tuple-element.12, f32[]{:T(128)} %bitcast.66, f32[]{:T(128)} %bitcast.65, f32[]{:T(128)} %bitcast.64, f32[1,1024]{1,0:T(1,128)} %param.8, f32[1,1040]{1,0:T(1,128)} %copy-done.14), kind=kLoop, calls=%fused_computation.336 | loop fusion | flops 6144 | bytes 20492 | tf_op jit(solution)/shard_map/broadcast_in_dim | solution.py:226
  123.3 4.5 %collective-permute-start.6 = (f32[1,1,8]{2,1,0:T(1,128)S(1)}, f32[1,1,8]{2,1,0:T(1,128)S(1)}, u32[]{:S(2)}, u32[]{:S(2)}) collective-permute-start(f32[1,1,8]{2,1,0:T(1,128)S(1)} %get-tuple-element.62), channel_id=1, source_target_pairs={{0,1},{1,2},{2,3},{3,4},{4,5},{5,6},{6,7},{8,9},{9,10},{10,11},{11... | collective-permute-start | bytes 104 | tf_op jit(solution)/shard_map/ppermute | solution.py:20
  136.8 41.8 %all-reduce.29 = (f32[4,32,64]{2,1,0:T(8,128)S(1)}, f32[3,16,32]{2,1,0:T(8,128)S(1)}, f32[32,16]{0,1:T(8,128)S(1)}, f32[7,32]{1,0:T(8,128)S(1)}) all-reduce(f32[4,32,64]{2,1,0:T(8,128)S(1)} %maximum_bitcast_fusion, f32[3,16,32]{2,1,0:T(8,128)S(1)} %maximum_bitcast_fusion.1, ...), channel_id=1, replica_groups=mesh['dp'=4,'tm'=8] {'dp','tm'}, use_global_device_ids=true, to_apply=%region_4.5 | all-reduce | flops 10464 | bytes 83712 | tf_op jit(solution)/shard_map/psum | solution.py:256
  (165 shorter events, 56.6 us)
Async XLA Ops:
  0.6 30.8 %copy-start = (f32[32,16]{0,1:T(8,128)S(1)}, f32[32,16]{0,1:T(8,128)}, u32[]{:S(2)}) copy-start(f32[32,16]{0,1:T(8,128)} %param.11) | copy-start | bytes 6148
  1.9 41.6 %collective-permute-start.3 = (f32[1,768]{1,0:T(1,128)}, f32[1,768]{1,0:T(1,128)}, u32[]{:S(2)}, u32[]{:S(2)}) collective-permute-start(f32[1,768]{1,0:T(1,128)} %slice.296), channel_id=1, source_target_pairs={{1,0},{2,1},{3,2},{4,3},{5,4},{6,5},{7,6},{9,8},{10,9},{11,10},{12... | collective-permute-start | bytes 9224 | tf_op jit(solution)/shard_map/ppermute | solution.py:32
  4.1 20.5 %collective-permute-start = (f32[1,64,4]{2,1,0:T(8,128)S(1)}, f32[1,64,4]{2,1,0:T(8,128)S(1)}, u32[]{:S(2)}, u32[]{:S(2)}) collective-permute-start(f32[1,64,4]{2,1,0:T(8,128)S(1)} %get-tuple-element.15), channel_id=1, source_target_pairs={{0,1},{1,2},{2,3},{3,4},{4,5},{5,6},{6,7},{8,9},{9,10},{10,11},{11... | collective-permute-start | bytes 3080 | tf_op jit(solution)/shard_map/ppermute | solution.py:20
  9.6 15.0 %collective-permute-start.1 = (f32[1,64,4]{2,1,0:T(8,128)S(1)}, f32[1,64,4]{2,1,0:T(8,128)S(1)}, u32[]{:S(2)}, u32[]{:S(2)}) collective-permute-start(f32[1,64,4]{2,1,0:T(8,128)S(1)} %get-tuple-element.16), channel_id=1, source_target_pairs={{1,0},{2,1},{3,2},{4,3},{5,4},{6,5},{7,6},{9,8},{10,9},{11,10},{12... | collective-permute-start | bytes 3080 | tf_op jit(solution)/shard_map/ppermute | solution.py:22
  15.1 9.5 %copy-start.7 = (f32[1,64,512]{2,1,0:T(8,128)S(1)}, f32[1,64,512]{2,1,0:T(8,128)}, u32[]{:S(2)}) copy-start(f32[1,64,512]{2,1,0:T(8,128)} %param.7) | copy-start | bytes 393220
  15.1 9.5 %copy-start.11 = (f32[4,32,64]{2,1,0:T(8,128)S(1)}, f32[4,32,64]{2,1,0:T(8,128)}, u32[]{:S(2)}) copy-start(f32[4,32,64]{2,1,0:T(8,128)} %param.9) | copy-start | bytes 98308
  32.7 5.9 %copy-start.9 = (f32[1,32,1040]{2,1,0:T(8,128)}, f32[1,32,1040]{2,1,0:T(8,128)S(1)}, u32[]{:S(2)}) copy-start(f32[1,32,1040]{2,1,0:T(8,128)S(1)} %get-tuple-element.74) | copy-start | bytes 399364
  42.3 14.1 %collective-permute-start.2 = (f32[1,768]{1,0:T(1,128)}, f32[1,768]{1,0:T(1,128)}, u32[]{:S(2)}, u32[]{:S(2)}) collective-permute-start(f32[1,768]{1,0:T(1,128)} %slice.333), channel_id=1, source_target_pairs={{1,0},{2,1},{3,2},{4,3},{5,4},{6,5},{7,6},{9,8},{10,9},{11,10},{12... | collective-permute-start | bytes 9224 | tf_op jit(solution)/shard_map/ppermute | solution.py:32
  51.1 4.3 %copy-start.2 = (f32[256,128]{1,0:T(8,128)S(1)}, f32[256,128]{1,0:T(8,128)}, u32[]{:S(2)}) copy-start(f32[256,128]{1,0:T(8,128)} %get-tuple-element.75) | copy-start | bytes 393220
  51.1 4.3 %copy-start.3 = (f32[256,128]{1,0:T(8,128)S(1)}, f32[256,128]{1,0:T(8,128)}, u32[]{:S(2)}) copy-start(f32[256,128]{1,0:T(8,128)} %get-tuple-element.76) | copy-start | bytes 393220
  51.1 5.2 %copy-start.16 = (f32[1,1024]{1,0:T(1,128)S(1)}, f32[1,1024]{1,0:T(1,128)}, u32[]{:S(2)}) copy-start(f32[1,1024]{1,0:T(1,128)} %get-tuple-element.53) | copy-start | bytes 12292
  71.7 20.1 %collective-permute-start.5 = (f32[1,768]{1,0:T(1,128)S(1)}, f32[1,768]{1,0:T(1,128)S(1)}, u32[]{:S(2)}, u32[]{:S(2)}) collective-permute-start(f32[1,768]{1,0:T(1,128)S(1)} %pad.112), channel_id=1, source_target_pairs={{0,1},{1,2},{2,3},{3,4},{4,5},{5,6},{6,7},{8,9},{9,10},{10,11},{11... | collective-permute-start | bytes 9224 | tf_op jit(solution)/shard_map/ppermute | solution.py:32
  78.0 3.7 %copy-start.23 = (f32[64]{0:T(128)S(1)}, f32[64]{0:T(128)}, u32[]{:S(2)}) copy-start(f32[64]{0:T(128)} %get-tuple-element.67) | copy-start | bytes 772
  78.0 3.7 %copy-start.24 = (f32[64]{0:T(128)S(1)}, f32[64]{0:T(128)}, u32[]{:S(2)}) copy-start(f32[64]{0:T(128)} %get-tuple-element.68) | copy-start | bytes 772
  78.0 4.1 %copy-start.22 = (f32[1,4,1024]{2,1,0:T(4,128)S(1)}, f32[1,4,1024]{2,1,0:T(4,128)}, u32[]{:S(2)}) copy-start(f32[1,4,1024]{2,1,0:T(4,128)} %fusion.15) | copy-start | bytes 49156
  83.3 8.6 %copy-start.21 = (f32[1,1216]{1,0:T(1,128)S(1)}, f32[1,1216]{1,0:T(1,128)}, u32[]{:S(2)}) copy-start(f32[1,1216]{1,0:T(1,128)} %reshape.974) | copy-start | bytes 14596
  86.8 43.6 %copy-start.10 = (f32[1,32,1040]{2,1,0:T(8,128)S(1)}, f32[1,32,1040]{2,1,0:T(8,128)}, u32[]{:S(2)}) copy-start(f32[1,32,1040]{2,1,0:T(8,128)} %copy-done.9) | copy-start | bytes 399364
  86.9 6.3 %collective-permute-start.4 = (f32[1,768]{1,0:T(1,128)S(1)}, f32[1,768]{1,0:T(1,128)S(1)}, u32[]{:S(2)}, u32[]{:S(2)}) collective-permute-start(f32[1,768]{1,0:T(1,128)S(1)} %slice.347), channel_id=1, source_target_pairs={{0,1},{1,2},{2,3},{3,4},{4,5},{5,6},{6,7},{8,9},{9,10},{10,11},{11... | collective-permute-start | bytes 9224 | tf_op jit(solution)/shard_map/ppermute | solution.py:32
  122.0 5.8 %collective-permute-start.7 = (f32[1,1,8]{2,1,0:T(1,128)S(1)}, f32[1,1,8]{2,1,0:T(1,128)S(1)}, u32[]{:S(2)}, u32[]{:S(2)}) collective-permute-start(f32[1,1,8]{2,1,0:T(1,128)S(1)} %get-tuple-element.61), channel_id=1, source_target_pairs={{1,0},{2,1},{3,2},{4,3},{5,4},{6,5},{7,6},{9,8},{10,9},{11,10},{12... | collective-permute-start | bytes 104 | tf_op jit(solution)/shard_map/ppermute | solution.py:22
  123.3 5.8 %collective-permute-start.6 = (f32[1,1,8]{2,1,0:T(1,128)S(1)}, f32[1,1,8]{2,1,0:T(1,128)S(1)}, u32[]{:S(2)}, u32[]{:S(2)}) collective-permute-start(f32[1,1,8]{2,1,0:T(1,128)S(1)} %get-tuple-element.62), channel_id=1, source_target_pairs={{0,1},{1,2},{2,3},{3,4},{4,5},{5,6},{6,7},{8,9},{9,10},{10,11},{11... | collective-permute-start | bytes 104 | tf_op jit(solution)/shard_map/ppermute | solution.py:20
  129.2 3.1 %copy-start.13 = (f32[3,16,32]{2,1,0:T(8,128)S(1)}, f32[3,16,32]{2,1,0:T(8,128)}, u32[]{:S(2)}) copy-start(f32[3,16,32]{2,1,0:T(8,128)} %param.10) | copy-start | bytes 18436
  131.2 2.7 %copy-start.5 = (f32[1,64,519]{2,1,0:T(8,128)S(1)}, f32[1,64,519]{2,1,0:T(8,128)}, u32[]{:S(2)}) copy-start(f32[1,64,519]{2,1,0:T(8,128)} %copy-done.4) | copy-start | bytes 398596
  131.7 2.7 %copy-start.8 = (f32[1,64,512]{2,1,0:T(8,128)S(1)}, f32[1,64,512]{2,1,0:T(8,128)}, u32[]{:S(2)}) copy-start(f32[1,64,512]{2,1,0:T(8,128)} %param.7) | copy-start | bytes 393220
  134.0 52.6 %copy-start.12 = (f32[4,32,64]{2,1,0:T(8,128)S(1)}, f32[4,32,64]{2,1,0:T(8,128)}, u32[]{:S(2)}) copy-start(f32[4,32,64]{2,1,0:T(8,128)} %param.9) | copy-start | bytes 98308
  (9 other events, 14.2 us)
where the time goes:
time: 190 us; the launch traced here: 188 us
  blocking collectives  63.8 us (34%)
  matrix products  37.6 us (20%)
  other arithmetic  31.8 us (17%)
  starting transfers between devices  26.4 us (14%)
  local copies, waits for them, and re-layouts  22 us (12%)
  between operations  4.65 us (2%)
  waiting for transfers between devices  1.95 us (1%)
    psum x1, blocking collectives, local(): lax.psum((local_totals[0], local_totals[1], local_totals[2], local_totals...  41.8 us
    dot_general x44, matrix products, product(): jnp.einsum(form, left, right, precision=lax.Precision.HIGHEST, preferred_...  37.6 us
    psum x1, blocking collectives, local(): squares = lax.psum(squares, 'tm')  22 us
    ppermute x4, starting transfers between devices, from_behind(): return lax.ppermute(x, axis, pairs)  13.8 us
    mul x2, other arithmetic, dft_table(): -hann_taper * jnp.sin(angles)  10.7 us
    ppermute x2, starting transfers between devices, padded_2(): lax.ppermute(tail, axis, [(i, (i + 1) % count) for i in range(ends)])  10.1 us
    reshape x5, local copies, waits for them, and re-layouts, framed(): blocks = signal.reshape(signal.shape[:-1] + (frame_count + 3, hop_size))  6.68 us
    slice x4, local copies, waits for them, and re-layouts, framed(): blocks[..., offset:offset + frame_count, :]  4.01 us
  transfers between devices with their start and end apart: 8, of which 2 were waited for; matrix products, arithmetic and copies ran while one was open for 28% of the time, Pallas kernels for 0%

commit v1 on v0

--- a/solution.py
+++ b/solution.py
@@ -253,9 +253,9 @@
         for member in (up_rows, inner_rows, outer_rows, out_rows)
     ]
     param_count = sum((member.size for member in local_totals))
-    summed = lax.psum(
-        (local_totals[0], local_totals[1], local_totals[2], local_totals[3]), ("dp", "tm")
-    )
+    summed = (local_totals[0], local_totals[1], local_totals[2], local_totals[3])
+    for mesh_axis in ("dp", "tm"):
+        summed = lax.psum(summed, mesh_axis)
     squares_all = sum((jnp.sum(member * member) for member in summed))
     factor = jnp.minimum(1.0, 1.0 / jnp.sqrt(squares_all / param_count + 1e-06))
     updates = [member * factor for member in summed]

time: 190 us -> 196 us (1.032)
  blocking collectives: 63.8 us -> 69.8 us
    psum x1 -> x2, blocking collectives: 41.8 us -> 47.9 us  [local(): summed = lax.psum(summed, mesh_axis)]
  transfers between devices with their start and end apart: 8 -> 8, of which waited for: 2 -> 2; matrix products, arithmetic and copies ran while one was open for 28% -> 27% of each run, Pallas kernels for 0% -> 0%
where the time goes in v1:
time: 196 us; the launch traced here: 194 us
  blocking collectives  69.8 us (36%)
  matrix products  37.6 us (19%)
  other arithmetic  31.8 us (16%)
  starting transfers between devices  26.4 us (13%)
  local copies, waits for them, and re-layouts  21.8 us (11%)
  between operations  4.69 us (2%)
    psum x2, blocking collectives, local(): summed = lax.psum(summed, mesh_axis)  47.9 us
    dot_general x44, matrix products, product(): jnp.einsum(form, left, right, precision=lax.Precision.HIGHEST, preferred_...  37.6 us
    psum x1, blocking collectives, local(): squares = lax.psum(squares, 'tm')  22 us
    ppermute x4, starting transfers between devices, from_behind(): return lax.ppermute(x, axis, pairs)  13.8 us
    mul x2, other arithmetic, dft_table(): -hann_taper * jnp.sin(angles)  10.7 us
    ppermute x2, starting transfers between devices, padded_2(): lax.ppermute(tail, axis, [(i, (i + 1) % count) for i in range(ends)])  10.1 us
    reshape x5, local copies, waits for them, and re-layouts, framed(): blocks = signal.reshape(signal.shape[:-1] + (frame_count + 3, hop_size))  6.68 us
    slice x4, local copies, waits for them, and re-layouts, framed(): blocks[..., offset:offset + frame_count, :]  4.01 us
  transfers between devices with their start and end apart: 8, of which 2 were waited for; matrix products, arithmetic and copies ran while one was open for 27% of the time, Pallas kernels for 0%

profile of v1, /device:TPU:0, one launch (start us, length us, event | category | flops | bytes accessed | tf_op | source)
XLA Modules:
  0.0 194.1 jit_solution(8169802335826273108)
XLA Ops:
  4.1 5.5 %collective-permute-start = (f32[1,64,4]{2,1,0:T(8,128)S(1)}, f32[1,64,4]{2,1,0:T(8,128)S(1)}, u32[]{:S(2)}, u32[]{:S(2)}) collective-permute-start(f32[1,64,4]{2,1,0:T(8,128)S(1)} %get-tuple-element.19), channel_id=1, source_target_pairs={{0,1},{1,2},{2,3},{3,4},{4,5},{5,6},{6,7},{8,9},{9,10},{10,11},{11... | collective-permute-start | bytes 3080 | tf_op jit(solution)/shard_map/ppermute | solution.py:20
  9.6 1.3 collective-permute-start.1
  12.3 1.6 slice_bitcast_fusion.6
  15.1 9.4 %sine_multiply_fusion = (f32[1024,512]{1,0:T(8,128)S(1)}, f32[1024,512]{1,0:T(8,128)}) fusion(f32[1024]{0:T(1024)S(1)} %fusion.218, f32[1024]{0:T(1024)S(1)} %multiply_subtract_fusion), kind=kLoop, calls=%fused_computation.21 | loop fusion | flops 8388608 | bytes 4202496 | tf_op jit(solution)/shard_map/jvp()/mul | solution.py:57
  39.5 2.0 %multiply_reduce_fusion.6 = (f32[]{:T(128)}, f32[1,1024]{1,0:T(1,128)}, f32[1,1792]{1,0:T(1,128)S(1)}) fusion(f32[1,1024]{1,0:T(1,128)} %param.8, f32[1,1040]{1,0:T(1,128)S(1)} %squeeze.11), kind=kLoop, calls=%fused_computation.340 | loop fusion | flops 4094 | bytes 16388 | tf_op jit(solution)/shard_map/reduce_sum | solution.py:220
  45.3 1.3 reduce.11
  47.9 1.4 reshape.970
  51.0 4.3 %fusion.15 = f32[1,4,1024]{2,1,0:T(4,128)} fusion(f32[1024,512]{1,0:T(8,128)S(1)} %get-tuple-element.81, f32[1024,512]{1,0:T(8,128)} %get-tuple-element.82, f32[1,4,256]{2,1,0:T(4,128)S(1)} %get-tuple-element.49, f32[1,4,256]{2,1,0:T(4,128)S(1)} %get-tuple-element.50, f32[1,4,256]{2,1,0:T(4,128)S(1)} %get-tuple-element.51, ...), kind=kOutput, calls=%fused_computation.33 | convolution fusion | flops 51392512 | bytes 4227072 | tf_op jit(solution)/shard_map/...nf,fk->...nk/dot_general | solution.py:36
  56.2 1.3 maximum_reduce_fusion
  57.5 1.3 reshape.959
  58.8 1.3 fusion.210
  60.1 1.4 reshape.967
  61.4 1.4 fusion.285
  69.5 1.4 reshape.974
  71.6 6.3 %collective-permute-start.5 = (f32[1,768]{1,0:T(1,128)S(1)}, f32[1,768]{1,0:T(1,128)S(1)}, u32[]{:S(2)}, u32[]{:S(2)}) collective-permute-start(f32[1,768]{1,0:T(1,128)S(1)} %pad.112), channel_id=1, source_target_pairs={{0,1},{1,2},{2,3},{3,4},{4,5},{5,6},{6,7},{8,9},{9,10},{10,11},{11... | collective-permute-start | bytes 9224 | tf_op jit(solution)/shard_map/ppermute | solution.py:32
  77.9 3.7 %fusion.14 = f32[1,4,1024]{2,1,0:T(4,128)S(1)} fusion(f32[1024,512]{1,0:T(8,128)S(1)} %get-tuple-element.81, f32[1024,512]{1,0:T(8,128)} %get-tuple-element.82, f32[1,4,256]{2,1,0:T(4,128)} %get-tuple-element.53, f32[1,4,256]{2,1,0:T(4,128)} %get-tuple-element.54, f32[1,4,256]{2,1,0:T(4,128)} %get-tuple-element.55, f32[1,4,256]{2,1,0:T(4,128)} %get-tuple-element.52), kind=kOutput, calls=%fused_computation.32 | convolution fusion | flops 51392512 | bytes 4227072 | tf_op jit(solution)/shard_map/jvp(...nf,fk->...nk)/dot_general | solution.py:36
  83.2 3.5 %fusion.16 = f32[1,4,1024]{2,1,0:T(4,128)S(1)} fusion(f32[1024,512]{1,0:T(8,128)S(1)} %get-tuple-element.81, f32[1024,512]{1,0:T(8,128)S(1)} %copy-done.1, f32[1,4,512]{2,1,0:T(4,128)S(1)} %get-tuple-element.22, f32[1,4,512]{2,1,0:T(4,128)S(1)} %get-tuple-element.21), kind=kOutput, calls=%fused_computation.34 | convolution fusion | flops 51384320 | bytes 4227072 | tf_op jit(solution)/shard_map/transpose(jvp(...nf,fk->...nk))/dot_general | solution.py:36
  86.8 5.0 %collective-permute-start.4 = (f32[1,768]{1,0:T(1,128)S(1)}, f32[1,768]{1,0:T(1,128)S(1)}, u32[]{:S(2)}, u32[]{:S(2)}) collective-permute-start(f32[1,768]{1,0:T(1,128)S(1)} %slice.347), channel_id=1, source_target_pairs={{0,1},{1,2},{2,3},{3,4},{4,5},{5,6},{6,7},{8,9},{9,10},{10,11},{11... | collective-permute-start | bytes 9224 | tf_op jit(solution)/shard_map/ppermute | solution.py:32
  93.7 2.0 %pad_maximum_fusion.16 = f32[1,3]{1,0:T(1,128)S(1)} fusion(f32[1,1]{1,0:T(1,128)} %bitcast.63, f32[1,1]{1,0:T(1,128)} %bitcast.53, f32[1,1]{1,0:T(1,128)} %bitcast.43), kind=kLoop, calls=%fused_computation.344 | loop fusion | flops 6 | bytes 24 | tf_op jit(solution)/shard_map/stack | solution.py:220
  95.8 22.0 %psum.63 = f32[1,3]{1,0:T(1,128)S(1)} all-reduce(f32[1,3]{1,0:T(1,128)S(1)} %pad_maximum_fusion.16), channel_id=1, replica_groups=mesh['dp'=4,'tm'=8] {'tm'}, use_global_device_ids=true, to_apply=%region_3.4 | all-reduce | flops 3 | bytes 24 | tf_op jit(solution)/shard_map/psum | solution.py:221
  119.7 2.1 %add_bitcast_fusion.1 = f32[1,1,1024]{2,1,0:T(1,128)S(1)} fusion(f32[1,1024]{1,0:T(1,128)S(1)} %get-tuple-element.18, f32[1,1024]{1,0:T(1,128)S(1)} %get-tuple-element.16, f32[]{:T(128)} %bitcast.66, f32[]{:T(128)} %bitcast.65, f32[]{:T(128)} %bitcast.64, f32[1,1024]{1,0:T(1,128)} %param.8, f32[1,1040]{1,0:T(1,128)} %copy-done.14), kind=kLoop, calls=%fused_computation.336 | loop fusion | flops 6144 | bytes 20492 | tf_op jit(solution)/shard_map/broadcast_in_dim | solution.py:226
  123.2 4.5 %collective-permute-start.6 = (f32[1,1,8]{2,1,0:T(1,128)S(1)}, f32[1,1,8]{2,1,0:T(1,128)S(1)}, u32[]{:S(2)}, u32[]{:S(2)}) collective-permute-start(f32[1,1,8]{2,1,0:T(1,128)S(1)} %get-tuple-element.66), channel_id=1, source_target_pairs={{0,1},{1,2},{2,3},{3,4},{4,5},{5,6},{6,7},{8,9},{9,10},{10,11},{11... | collective-permute-start | bytes 104 | tf_op jit(solution)/shard_map/ppermute | solution.py:20
  136.7 11.3 %all-reduce.30 = (f32[4,32,64]{2,1,0:T(8,128)S(1)}, f32[3,16,32]{2,1,0:T(8,128)S(1)}, f32[32,16]{0,1:T(8,128)S(1)}, f32[7,32]{1,0:T(8,128)S(1)}) all-reduce(f32[4,32,64]{2,1,0:T(8,128)S(1)} %maximum_bitcast_fusion, f32[3,16,32]{2,1,0:T(8,128)S(1)} %maximum_bitcast_fusion.1, ...), channel_id=1, replica_groups=mesh['dp'=4,'tm'=8] {'dp'}, use_global_device_ids=true, to_apply=%region_4.5 | all-reduce | flops 10464 | bytes 83712 | tf_op jit(solution)/shard_map/psum | solution.py:258
  148.0 36.5 %all-reduce.29 = (f32[4,32,64]{2,1,0:T(8,128)S(1)}, f32[3,16,32]{2,1,0:T(8,128)S(1)}, f32[32,16]{0,1:T(8,128)S(1)}, f32[7,32]{1,0:T(8,128)S(1)}) all-reduce(f32[4,32,64]{2,1,0:T(8,128)S(1)} %get-tuple-element.9, f32[3,16,32]{2,1,0:T(8,128)S(1)} %get-tuple-element.10, ...), channel_id=1, replica_groups=mesh['dp'=4,'tm'=8] {'tm'}, use_global_device_ids=true, to_apply=%region_5.6 | all-reduce | flops 10464 | bytes 83712 | tf_op jit(solution)/shard_map/psum | solution.py:258
  (166 shorter events, 57.7 us)
Async XLA Ops:
  0.6 30.6 %copy-start = (f32[32,16]{0,1:T(8,128)S(1)}, f32[32,16]{0,1:T(8,128)}, u32[]{:S(2)}) copy-start(f32[32,16]{0,1:T(8,128)} %param.11) | copy-start | bytes 6148
  1.9 41.5 %collective-permute-start.3 = (f32[1,768]{1,0:T(1,128)}, f32[1,768]{1,0:T(1,128)}, u32[]{:S(2)}, u32[]{:S(2)}) collective-permute-start(f32[1,768]{1,0:T(1,128)} %slice.296), channel_id=1, source_target_pairs={{1,0},{2,1},{3,2},{4,3},{5,4},{6,5},{7,6},{9,8},{10,9},{11,10},{12... | collective-permute-start | bytes 9224 | tf_op jit(solution)/shard_map/ppermute | solution.py:32
  4.1 20.5 %collective-permute-start = (f32[1,64,4]{2,1,0:T(8,128)S(1)}, f32[1,64,4]{2,1,0:T(8,128)S(1)}, u32[]{:S(2)}, u32[]{:S(2)}) collective-permute-start(f32[1,64,4]{2,1,0:T(8,128)S(1)} %get-tuple-element.19), channel_id=1, source_target_pairs={{0,1},{1,2},{2,3},{3,4},{4,5},{5,6},{6,7},{8,9},{9,10},{10,11},{11... | collective-permute-start | bytes 3080 | tf_op jit(solution)/shard_map/ppermute | solution.py:20
  9.6 15.0 %collective-permute-start.1 = (f32[1,64,4]{2,1,0:T(8,128)S(1)}, f32[1,64,4]{2,1,0:T(8,128)S(1)}, u32[]{:S(2)}, u32[]{:S(2)}) collective-permute-start(f32[1,64,4]{2,1,0:T(8,128)S(1)} %get-tuple-element.20), channel_id=1, source_target_pairs={{1,0},{2,1},{3,2},{4,3},{5,4},{6,5},{7,6},{9,8},{10,9},{11,10},{12... | collective-permute-start | bytes 3080 | tf_op jit(solution)/shard_map/ppermute | solution.py:22
  15.1 9.5 %copy-start.7 = (f32[1,64,512]{2,1,0:T(8,128)S(1)}, f32[1,64,512]{2,1,0:T(8,128)}, u32[]{:S(2)}) copy-start(f32[1,64,512]{2,1,0:T(8,128)} %param.7) | copy-start | bytes 393220
  15.1 9.5 %copy-start.11 = (f32[4,32,64]{2,1,0:T(8,128)S(1)}, f32[4,32,64]{2,1,0:T(8,128)}, u32[]{:S(2)}) copy-start(f32[4,32,64]{2,1,0:T(8,128)} %param.9) | copy-start | bytes 98308
  32.6 5.9 %copy-start.9 = (f32[1,32,1040]{2,1,0:T(8,128)}, f32[1,32,1040]{2,1,0:T(8,128)S(1)}, u32[]{:S(2)}) copy-start(f32[1,32,1040]{2,1,0:T(8,128)S(1)} %get-tuple-element.78) | copy-start | bytes 399364
  42.1 14.1 %collective-permute-start.2 = (f32[1,768]{1,0:T(1,128)}, f32[1,768]{1,0:T(1,128)}, u32[]{:S(2)}, u32[]{:S(2)}) collective-permute-start(f32[1,768]{1,0:T(1,128)} %slice.333), channel_id=1, source_target_pairs={{1,0},{2,1},{3,2},{4,3},{5,4},{6,5},{7,6},{9,8},{10,9},{11,10},{12... | collective-permute-start | bytes 9224 | tf_op jit(solution)/shard_map/ppermute | solution.py:32
  51.0 4.3 %copy-start.2 = (f32[256,128]{1,0:T(8,128)S(1)}, f32[256,128]{1,0:T(8,128)}, u32[]{:S(2)}) copy-start(f32[256,128]{1,0:T(8,128)} %get-tuple-element.79) | copy-start | bytes 393220
  51.0 4.3 %copy-start.3 = (f32[256,128]{1,0:T(8,128)S(1)}, f32[256,128]{1,0:T(8,128)}, u32[]{:S(2)}) copy-start(f32[256,128]{1,0:T(8,128)} %get-tuple-element.80) | copy-start | bytes 393220
  51.0 5.2 %copy-start.16 = (f32[1,1024]{1,0:T(1,128)S(1)}, f32[1,1024]{1,0:T(1,128)}, u32[]{:S(2)}) copy-start(f32[1,1024]{1,0:T(1,128)} %get-tuple-element.57) | copy-start | bytes 12292
  71.6 20.2 %collective-permute-start.5 = (f32[1,768]{1,0:T(1,128)S(1)}, f32[1,768]{1,0:T(1,128)S(1)}, u32[]{:S(2)}, u32[]{:S(2)}) collective-permute-start(f32[1,768]{1,0:T(1,128)S(1)} %pad.112), channel_id=1, source_target_pairs={{0,1},{1,2},{2,3},{3,4},{4,5},{5,6},{6,7},{8,9},{9,10},{10,11},{11... | collective-permute-start | bytes 9224 | tf_op jit(solution)/shard_map/ppermute | solution.py:32
  77.8 3.7 %copy-start.23 = (f32[64]{0:T(128)S(1)}, f32[64]{0:T(128)}, u32[]{:S(2)}) copy-start(f32[64]{0:T(128)} %get-tuple-element.71) | copy-start | bytes 772
  77.9 3.7 %copy-start.24 = (f32[64]{0:T(128)S(1)}, f32[64]{0:T(128)}, u32[]{:S(2)}) copy-start(f32[64]{0:T(128)} %get-tuple-element.72) | copy-start | bytes 772
  77.9 4.1 %copy-start.22 = (f32[1,4,1024]{2,1,0:T(4,128)S(1)}, f32[1,4,1024]{2,1,0:T(4,128)}, u32[]{:S(2)}) copy-start(f32[1,4,1024]{2,1,0:T(4,128)} %fusion.15) | copy-start | bytes 49156
  83.2 8.6 %copy-start.21 = (f32[1,1216]{1,0:T(1,128)S(1)}, f32[1,1216]{1,0:T(1,128)}, u32[]{:S(2)}) copy-start(f32[1,1216]{1,0:T(1,128)} %reshape.974) | copy-start | bytes 14596
  86.7 43.6 %copy-start.10 = (f32[1,32,1040]{2,1,0:T(8,128)S(1)}, f32[1,32,1040]{2,1,0:T(8,128)}, u32[]{:S(2)}) copy-start(f32[1,32,1040]{2,1,0:T(8,128)} %copy-done.9) | copy-start | bytes 399364
  86.8 6.3 %collective-permute-start.4 = (f32[1,768]{1,0:T(1,128)S(1)}, f32[1,768]{1,0:T(1,128)S(1)}, u32[]{:S(2)}, u32[]{:S(2)}) collective-permute-start(f32[1,768]{1,0:T(1,128)S(1)} %slice.347), channel_id=1, source_target_pairs={{0,1},{1,2},{2,3},{3,4},{4,5},{5,6},{6,7},{8,9},{9,10},{10,11},{11... | collective-permute-start | bytes 9224 | tf_op jit(solution)/shard_map/ppermute | solution.py:32
  121.9 5.8 %collective-permute-start.7 = (f32[1,1,8]{2,1,0:T(1,128)S(1)}, f32[1,1,8]{2,1,0:T(1,128)S(1)}, u32[]{:S(2)}, u32[]{:S(2)}) collective-permute-start(f32[1,1,8]{2,1,0:T(1,128)S(1)} %get-tuple-element.65), channel_id=1, source_target_pairs={{1,0},{2,1},{3,2},{4,3},{5,4},{6,5},{7,6},{9,8},{10,9},{11,10},{12... | collective-permute-start | bytes 104 | tf_op jit(solution)/shard_map/ppermute | solution.py:22
  123.2 5.8 %collective-permute-start.6 = (f32[1,1,8]{2,1,0:T(1,128)S(1)}, f32[1,1,8]{2,1,0:T(1,128)S(1)}, u32[]{:S(2)}, u32[]{:S(2)}) collective-permute-start(f32[1,1,8]{2,1,0:T(1,128)S(1)} %get-tuple-element.66), channel_id=1, source_target_pairs={{0,1},{1,2},{2,3},{3,4},{4,5},{5,6},{6,7},{8,9},{9,10},{10,11},{11... | collective-permute-start | bytes 104 | tf_op jit(solution)/shard_map/ppermute | solution.py:20
  129.1 3.1 %copy-start.13 = (f32[3,16,32]{2,1,0:T(8,128)S(1)}, f32[3,16,32]{2,1,0:T(8,128)}, u32[]{:S(2)}) copy-start(f32[3,16,32]{2,1,0:T(8,128)} %param.10) | copy-start | bytes 18436
  131.1 2.8 %copy-start.5 = (f32[1,64,519]{2,1,0:T(8,128)S(1)}, f32[1,64,519]{2,1,0:T(8,128)}, u32[]{:S(2)}) copy-start(f32[1,64,519]{2,1,0:T(8,128)} %copy-done.4) | copy-start | bytes 398596
  131.5 2.7 %copy-start.8 = (f32[1,64,512]{2,1,0:T(8,128)S(1)}, f32[1,64,512]{2,1,0:T(8,128)}, u32[]{:S(2)}) copy-start(f32[1,64,512]{2,1,0:T(8,128)} %param.7) | copy-start | bytes 393220
  133.8 58.7 %copy-start.12 = (f32[4,32,64]{2,1,0:T(8,128)S(1)}, f32[4,32,64]{2,1,0:T(8,128)}, u32[]{:S(2)}) copy-start(f32[4,32,64]{2,1,0:T(8,128)} %param.9) | copy-start | bytes 98308
  (9 other events, 17.0 us)
